TPU v7x, 512 devices: a whole 4x8x8 slice. The times are simulated.
512 devices in a mesh: rep: 16 (over x, y_lo), shard: 32 (over z, y_hi, core).
Axes of the slice: x: 4, y: 8 (y_hi: 2, y_lo: 4; y = y_hi * 4 + y_lo), z: 8, core: 2. Of those that a mesh axis runs over, the one named last changes fastest.
Arguments:
- inner_weights: float32 [16, 2, 512, 512], P('rep', None, 'shard'), may hold values from -6 to 6
- first_moment: float32 [16, 2, 512, 512], P('rep', None, 'shard'), may hold values from -1 to 1
- second_moment: float32 [16, 2, 512, 512], P('rep', None, 'shard'), may hold values from 0 to 1, as said below
- outer_weights: float32 [2, 512, 512], P(None, 'shard'), may hold values from -6 to 6
- outer_velocity: float32 [2, 512, 512], P(None, 'shard'), may hold values from -3 to 3
- tokens: bfloat16 [16, 2, 16384, 512], P('rep', None, 'shard'), may hold values from -6 to 6
- targets: bfloat16 [16, 2, 16384, 2, 512], P('rep', None, 'shard'), may hold values from -25 to 25
- step_count: int32 [1], replicated, may hold values from 10 to 39
- first_fragment: int32 [1], replicated, may hold values from 0 to 1
Outputs:
- new_outer: float32 [2, 512, 512], P(None, 'shard')
- new_inner: float32 [16, 2, 512, 512], P('rep', None, 'shard')
Inputs may be any that keep to these rules, and one draw needn't show every extreme that they name: `second_moment`: positive.
All inputs are finite; a program needn't handle non-finite values.
Results may differ from a plain program's by a relative error of at most 0.00085.
Values may be sent and summed in bfloat16 or wider, within the bound.
A program may use at most 64 MiB of HBM per device.

v0:
```python
import math

import jax
import jax.numpy as jnp
from jax import lax
from jax.sharding import PartitionSpec as P

beta_one = 0.9
beta_two = 0.95
inner_rate = 0.1
adam_eps = 1e-08
decay_rate = 0.1
clip_norm = 0.02
outer_rate = 0.7
outer_momentum = 0.9
mixing = 0.5


def from_everyone(x, axis):
    peers = lax.axis_size(axis)
    return lax.all_to_all(jnp.broadcast_to(x[None], (peers, *x.shape)), axis, 0, 0, tiled=True)


def laid_out(tiles, dim):
    shape = list(tiles.shape[1:])
    shape[dim] *= tiles.shape[0]
    return jnp.moveaxis(tiles, 0, dim).reshape(shape)


def collect(x, axis, dim):
    tiles = from_everyone(x, axis)
    return laid_out(tiles, dim)


def in_blocks(x, dim, peers):
    before, after = (x.shape[:dim], x.shape[dim + 1 :])
    return jnp.moveaxis(x.reshape(*before, peers, -1, *after), dim, 0)


def sum_at_owner(x, axis, dim):
    peers = lax.axis_size(axis)
    tiles = lax.all_to_all(in_blocks(x, dim, peers), axis, 0, 0, tiled=True)
    return jnp.sum(tiles.astype(jnp.float32), axis=0)


def of_everyone(x, axis):
    everything = from_everyone(x, axis)
    return jnp.sum(everything, axis=0)


def body(
    inner_weights,
    first_moment,
    second_moment,
    outer_weights,
    outer_velocity,
    tokens,
    targets,
    step_count,
    first_fragment,
):
    weights = inner_weights[0]
    moment_one = first_moment[0]
    moment_two = second_moment[0]
    outer = outer_weights
    velocity = outer_velocity
    width = weights.shape[2]
    replicas = lax.axis_size("rep")
    shards = lax.axis_size("shard")
    tok_dev = tokens.shape[2]
    scale = 1.0 / math.sqrt(width)
    grad_scale = scale / (tok_dev * shards)
    first = first_fragment[0]
    for step in range(tokens.shape[1]):
        frag = first if step == 0 else 1 - first
        theta = lax.dynamic_index_in_dim(outer, frag, 0, keepdims=False)
        speed = lax.dynamic_index_in_dim(velocity, frag, 0, keepdims=False)
        own = lax.dynamic_index_in_dim(weights, frag, 0, keepdims=False)
        batch = tokens[0, step]
        target = targets[0, step]
        lowered = weights.astype(jnp.bfloat16)
        raw = jnp.einsum(
            "td,fkd->tfk", batch, collect(lowered, "shard", 1), preferred_element_type=jnp.float32
        )
        residual = (raw * scale - target.astype(jnp.float32)).astype(jnp.bfloat16)
        partial_grad = (
            jnp.einsum("tfk,td->fkd", residual, batch, preferred_element_type=jnp.float32)
            * grad_scale
        )
        grad = sum_at_owner(partial_grad.astype(jnp.bfloat16), "shard", 1)
        summed = of_everyone(theta - own, "rep")
        delta = summed / replicas
        speed = outer_momentum * speed + delta
        theta = theta - outer_rate * (outer_momentum * speed + delta)
        outer = lax.dynamic_update_index_in_dim(outer, theta, frag, 0)
        velocity = lax.dynamic_update_index_in_dim(velocity, speed, frag, 0)
        squares = of_everyone(jnp.sum(grad * grad), "shard")
        norm = jnp.sqrt(squares)
        clipped = grad * jnp.minimum(1.0, clip_norm / (norm + 1e-06))
        count = step_count[0].astype(jnp.float32) + step
        moment_one = beta_one * moment_one + (1.0 - beta_one) * clipped
        moment_two = beta_two * moment_two + (1.0 - beta_two) * clipped * clipped
        correct_one = 1.0 - jnp.power(beta_one, count)
        correct_two = 1.0 - jnp.power(beta_two, count)
        update = moment_one / correct_one / (jnp.sqrt(moment_two / correct_two) + adam_eps)
        weights = weights - inner_rate * (update + decay_rate * weights)
        local = lax.dynamic_index_in_dim(weights, frag, 0, keepdims=False)
        merged = mixing * theta + (1.0 - mixing) * local
        weights = lax.dynamic_update_index_in_dim(weights, merged, frag, 0)
    return (outer, weights[None])


def solution(mesh):
    in_specs = (
        P("rep", None, "shard", None),
        P("rep", None, "shard", None),
        P("rep", None, "shard", None),
        P(None, "shard", None),
        P(None, "shard", None),
        P("rep", None, "shard", None),
        P("rep", None, "shard", None, None),
        P(),
        P(),
    )
    out_specs = (P(None, "shard", None), P("rep", None, "shard", None))
    return jax.shard_map(body, mesh=mesh, in_specs=in_specs, out_specs=out_specs, check_vma=False)
```

profile of v0, /device:TPU:1, one launch (start us, length us, event | category | flops | bytes accessed | tf_op | source)
XLA Modules:
  0.0 260.7 jit_solution(307725486677049742)
XLA Ops:
  0.6 0.8 copy.60
  1.5 0.8 convert_bitcast_fusion
  2.3 1.1 broadcast_in_dim.56
  3.4 17.2 %all-to-all-start.1 = ((bf16[32,2,16,512]{3,2,1,0:T(8,128)(2,1)}), bf16[32,2,16,512]{3,2,1,0:T(8,128)(2,1)S(1)}, u32[]{:S(2)}, u32[]{:S(2)}) async-start(bf16[32,2,16,512]{3,2,1,0:T(8,128)(2,1)} %broadcast_in_dim.56), calls=%async_computation.1 | async-start | bytes 2097152 | tf_op jit(solution)/shard_map/all_to_all | solution.py:21
  20.7 3.5 %fusion.31 = (bf16[1,1,512,2,512]{4,3,2,1,0:T(2,128)(2,1)S(1)}, bf16[1,1,512,2,512]{4,3,2,1,0:T(2,128)(2,1)}) fusion(bf16[1,2,512,2,512]{4,3,2,1,0:T(2,128)(2,1)} %param.15), kind=kLoop, calls=%fused_computation.55 | loop fusion | bytes 4194304 | tf_op jit(solution)/shard_map/slice | solution.py:80
  24.1 26.9 %all-to-all-done.1 = bf16[32,2,16,512]{3,2,1,0:T(8,128)(2,1)S(1)} async-done(((bf16[32,2,16,512]{3,2,1,0:T(8,128)(2,1)}), bf16[32,2,16,512]{3,2,1,0:T(8,128)(2,1)S(1)}, u32[]{:S(2)}, u32[]{:S(2)}) %all-to-all-start.1) | async-done | bytes 1048608 | tf_op jit(solution)/shard_map/all_to_all | solution.py:21
  51.0 0.1 copy.29
  51.1 3.0 %multiply_convert_fusion.1 = bf16[2,512,512]{2,1,0:T(8,128)(2,1)S(1)} fusion(bf16[2,512,512]{2,1,0:T(8,128)(2,1)S(1)} %bitcast.118, bf16[1,1,512,2,512]{4,3,2,1,0:T(2,128)(2,1)} %get-tuple-element.3, bf16[1,2,512,512]{3,2,1,0:T(8,128)(2,1)} %param.14), kind=kOutput, calls=%fused_computation.7 | convolution fusion | flops 1076887552 | bytes 4194304 | tf_op jit(solution)/shard_map/tfk,td->fkd/dot_general | solution.py:87
  54.1 0.0 copy-start.2
  54.1 1.1 copy.50
  55.2 6.3 %all-to-all-start.2 = ((bf16[32,2,16,512]{3,2,1,0:T(8,128)(2,1)}), bf16[32,2,16,512]{3,2,1,0:T(8,128)(2,1)S(1)}, u32[]{:S(2)}, u32[]{:S(2)}) async-start(bf16[32,2,16,512]{3,2,1,0:T(8,128)(2,1)} %bitcast.112), calls=%async_computation.2 | async-start | bytes 2097152 | tf_op jit(solution)/shard_map/all_to_all | solution.py:42
  61.5 0.0 copy-start.4
  61.5 0.0 copy-start.5
  61.5 0.0 copy-start.3
  62.2 0.0 copy-done.2
  62.3 27.9 %all-to-all-done.2 = bf16[32,2,16,512]{3,2,1,0:T(8,128)(2,1)S(1)} async-done(((bf16[32,2,16,512]{3,2,1,0:T(8,128)(2,1)}), bf16[32,2,16,512]{3,2,1,0:T(8,128)(2,1)S(1)}, u32[]{:S(2)}, u32[]{:S(2)}) %all-to-all-start.2) | async-done | bytes 1048608 | tf_op jit(solution)/shard_map/all_to_all | solution.py:42
  90.2 0.8 broadcast_in_dim.54
  91.0 9.7 %all-to-all-start = ((f32[16,16,512]{2,1,0:T(8,128)}), f32[16,16,512]{2,1,0:T(8,128)S(1)}, u32[]{:S(2)}, u32[]{:S(2)}) async-start(f32[16,16,512]{2,1,0:T(8,128)} %broadcast_in_dim.54), calls=%async_computation | async-start | bytes 1048576 | tf_op jit(solution)/shard_map/all_to_all | solution.py:21
  101.5 0.2 convert_reduce_fusion.1
  101.6 0.7 multiply_reduce_fusion.1
  102.3 13.9 %all-to-all-done = f32[16,16,512]{2,1,0:T(8,128)S(1)} async-done(((f32[16,16,512]{2,1,0:T(8,128)}), f32[16,16,512]{2,1,0:T(8,128)S(1)}, u32[]{:S(2)}, u32[]{:S(2)}) %all-to-all-start) | async-done | bytes 524320 | tf_op jit(solution)/shard_map/all_to_all | solution.py:21
  116.2 1.2 broadcast_in_dim.57
  117.5 7.4 %all-to-all-start.3 = ((f32[32,1,1]{2,1,0:T(1,128)}), f32[32,1,1]{2,1,0:T(1,128)S(1)}, u32[]{:S(2)}, u32[]{:S(2)}) async-start(f32[32,1,1]{2,1,0:T(1,128)} %broadcast_in_dim.57), calls=%async_computation.3 | async-start | bytes 32768 | tf_op jit(solution)/shard_map/all_to_all | solution.py:21
  124.9 11.6 %all-to-all-done.3 = f32[32,1,1]{2,1,0:T(1,128)S(1)} async-done(((f32[32,1,1]{2,1,0:T(1,128)}), f32[32,1,1]{2,1,0:T(1,128)S(1)}, u32[]{:S(2)}, u32[]{:S(2)}) %all-to-all-start.3) | async-done | bytes 160 | tf_op jit(solution)/shard_map/all_to_all | solution.py:21
  136.5 0.6 reduce_sum.75
  137.9 0.0 copy-done.4
  137.9 0.0 copy-done.5
  137.9 0.1 bitcast_subtract_fusion
  138.0 0.0 copy-done.3
  138.1 1.1 broadcast_in_dim.60
  139.2 4.2 %all-to-all-start.5 = ((bf16[32,2,16,512]{3,2,1,0:T(8,128)(2,1)}), bf16[32,2,16,512]{3,2,1,0:T(8,128)(2,1)S(1)}, u32[]{:S(2)}, u32[]{:S(2)}) async-start(bf16[32,2,16,512]{3,2,1,0:T(8,128)(2,1)} %broadcast_in_dim.60), calls=%async_computation.5 | async-start | bytes 2097152 | tf_op jit(solution)/shard_map/all_to_all | solution.py:21
  143.4 2.5 copy.42
  145.9 0.0 copy-start
  145.9 27.7 %all-to-all-done.5 = bf16[32,2,16,512]{3,2,1,0:T(8,128)(2,1)S(1)} async-done(((bf16[32,2,16,512]{3,2,1,0:T(8,128)(2,1)}), bf16[32,2,16,512]{3,2,1,0:T(8,128)(2,1)S(1)}, u32[]{:S(2)}, u32[]{:S(2)}) %all-to-all-start.5) | async-done | bytes 1048608 | tf_op jit(solution)/shard_map/all_to_all | solution.py:21
  173.6 0.1 copy.34
  173.7 0.0 copy-done
  173.7 2.5 multiply_convert_fusion
  176.2 1.1 copy.49
  177.3 8.5 %all-to-all-start.6 = ((bf16[32,2,16,512]{3,2,1,0:T(8,128)(2,1)}), bf16[32,2,16,512]{3,2,1,0:T(8,128)(2,1)S(1)}, u32[]{:S(2)}, u32[]{:S(2)}) async-start(bf16[32,2,16,512]{3,2,1,0:T(8,128)(2,1)} %bitcast.111), calls=%async_computation.6 | async-start | bytes 2097152 | tf_op jit(solution)/shard_map/all_to_all | solution.py:42
  185.8 27.9 %all-to-all-done.6 = bf16[32,2,16,512]{3,2,1,0:T(8,128)(2,1)S(1)} async-done(((bf16[32,2,16,512]{3,2,1,0:T(8,128)(2,1)}), bf16[32,2,16,512]{3,2,1,0:T(8,128)(2,1)S(1)}, u32[]{:S(2)}, u32[]{:S(2)}) %all-to-all-start.6) | async-done | bytes 1048608 | tf_op jit(solution)/shard_map/all_to_all | solution.py:42
  213.7 0.8 broadcast_in_dim.59
  214.6 5.9 %all-to-all-start.4 = ((f32[16,16,512]{2,1,0:T(8,128)}), f32[16,16,512]{2,1,0:T(8,128)S(1)}, u32[]{:S(2)}, u32[]{:S(2)}) async-start(f32[16,16,512]{2,1,0:T(8,128)} %broadcast_in_dim.59), calls=%async_computation.4 | async-start | bytes 1048576 | tf_op jit(solution)/shard_map/all_to_all | solution.py:21
  220.5 0.2 convert_reduce_fusion
  220.6 0.6 multiply_reduce_fusion
  221.2 14.7 %all-to-all-done.4 = f32[16,16,512]{2,1,0:T(8,128)S(1)} async-done(((f32[16,16,512]{2,1,0:T(8,128)}), f32[16,16,512]{2,1,0:T(8,128)S(1)}, u32[]{:S(2)}, u32[]{:S(2)}) %all-to-all-start.4) | async-done | bytes 524320 | tf_op jit(solution)/shard_map/all_to_all | solution.py:21
  235.9 1.3 broadcast_in_dim.61
  237.2 9.0 %all-to-all-start.7 = ((f32[32,1,1]{2,1,0:T(1,128)}), f32[32,1,1]{2,1,0:T(1,128)S(1)}, u32[]{:S(2)}, u32[]{:S(2)}) async-start(f32[32,1,1]{2,1,0:T(1,128)} %broadcast_in_dim.61), calls=%async_computation.7 | async-start | bytes 32768 | tf_op jit(solution)/shard_map/all_to_all | solution.py:21
  246.4 11.5 %all-to-all-done.7 = f32[32,1,1]{2,1,0:T(1,128)S(1)} async-done(((f32[32,1,1]{2,1,0:T(1,128)}), f32[32,1,1]{2,1,0:T(1,128)S(1)}, u32[]{:S(2)}, u32[]{:S(2)}) %all-to-all-start.7) | async-done | bytes 160 | tf_op jit(solution)/shard_map/all_to_all | solution.py:21
  257.9 0.6 reduce_sum.79
  259.3 0.1 multiply_subtract_fusion
  259.4 0.0 copy-start.6
  259.5 0.6 copy-done.6
  260.0 0.0 copy-start.1
  260.1 0.6 copy-done.1
  (9 shorter events, 0.2 us)
Async XLA Ops:
  3.4 47.5 %all-to-all-start.1 = ((bf16[32,2,16,512]{3,2,1,0:T(8,128)(2,1)}), bf16[32,2,16,512]{3,2,1,0:T(8,128)(2,1)S(1)}, u32[]{:S(2)}, u32[]{:S(2)}) async-start(bf16[32,2,16,512]{3,2,1,0:T(8,128)(2,1)} %broadcast_in_dim.56), calls=%async_computation.1 | async-start | bytes 2097152 | tf_op jit(solution)/shard_map/all_to_all | solution.py:21
  54.1 8.2 %copy-start.2 = (f32[1,2,16,512]{3,2,1,0:T(8,128)S(1)}, f32[1,2,16,512]{3,2,1,0:T(8,128)}, u32[]{:S(2)}) copy-start(f32[1,2,16,512]{3,2,1,0:T(8,128)} %param.9) | copy-start | bytes 196612
  55.2 35.0 %all-to-all-start.2 = ((bf16[32,2,16,512]{3,2,1,0:T(8,128)(2,1)}), bf16[32,2,16,512]{3,2,1,0:T(8,128)(2,1)S(1)}, u32[]{:S(2)}, u32[]{:S(2)}) async-start(bf16[32,2,16,512]{3,2,1,0:T(8,128)(2,1)} %bitcast.112), calls=%async_computation.2 | async-start | bytes 2097152 | tf_op jit(solution)/shard_map/all_to_all | solution.py:42
  61.5 76.4 %copy-start.4 = (f32[1,2,16,512]{3,2,1,0:T(8,128)S(1)}, f32[1,2,16,512]{3,2,1,0:T(8,128)}, u32[]{:S(2)}) copy-start(f32[1,2,16,512]{3,2,1,0:T(8,128)} %param.10) | copy-start | bytes 196612
  61.5 76.4 %copy-start.5 = (f32[1,2,16,512]{3,2,1,0:T(8,128)S(1)}, f32[1,2,16,512]{3,2,1,0:T(8,128)}, u32[]{:S(2)}) copy-start(f32[1,2,16,512]{3,2,1,0:T(8,128)} %param.11) | copy-start | bytes 196612
  61.5 76.5 %copy-start.3 = (f32[2,16,512]{2,1,0:T(8,128)S(1)}, f32[2,16,512]{2,1,0:T(8,128)}, u32[]{:S(2)}) copy-start(f32[2,16,512]{2,1,0:T(8,128)} %param.13) | copy-start | bytes 196612
  91.0 25.2 %all-to-all-start = ((f32[16,16,512]{2,1,0:T(8,128)}), f32[16,16,512]{2,1,0:T(8,128)S(1)}, u32[]{:S(2)}, u32[]{:S(2)}) async-start(f32[16,16,512]{2,1,0:T(8,128)} %broadcast_in_dim.54), calls=%async_computation | async-start | bytes 1048576 | tf_op jit(solution)/shard_map/all_to_all | solution.py:21
  117.5 19.1 %all-to-all-start.3 = ((f32[32,1,1]{2,1,0:T(1,128)}), f32[32,1,1]{2,1,0:T(1,128)S(1)}, u32[]{:S(2)}, u32[]{:S(2)}) async-start(f32[32,1,1]{2,1,0:T(1,128)} %broadcast_in_dim.57), calls=%async_computation.3 | async-start | bytes 32768 | tf_op jit(solution)/shard_map/all_to_all | solution.py:21
  139.2 34.4 %all-to-all-start.5 = ((bf16[32,2,16,512]{3,2,1,0:T(8,128)(2,1)}), bf16[32,2,16,512]{3,2,1,0:T(8,128)(2,1)S(1)}, u32[]{:S(2)}, u32[]{:S(2)}) async-start(bf16[32,2,16,512]{3,2,1,0:T(8,128)(2,1)} %broadcast_in_dim.60), calls=%async_computation.5 | async-start | bytes 2097152 | tf_op jit(solution)/shard_map/all_to_all | solution.py:21
  145.9 27.8 %copy-start = (bf16[1,1,512,2,512]{2,4,3,1,0:T(8,128)(2,1)S(1)}, bf16[1,1,512,2,512]{2,4,3,1,0:T(8,128)(2,1)}, u32[]{:S(2)}) copy-start(bf16[1,1,512,2,512]{2,4,3,1,0:T(8,128)(2,1)} %copy.42) | copy-start | bytes 3145732
  177.3 36.5 %all-to-all-start.6 = ((bf16[32,2,16,512]{3,2,1,0:T(8,128)(2,1)}), bf16[32,2,16,512]{3,2,1,0:T(8,128)(2,1)S(1)}, u32[]{:S(2)}, u32[]{:S(2)}) async-start(bf16[32,2,16,512]{3,2,1,0:T(8,128)(2,1)} %bitcast.111), calls=%async_computation.6 | async-start | bytes 2097152 | tf_op jit(solution)/shard_map/all_to_all | solution.py:42
  214.6 21.3 %all-to-all-start.4 = ((f32[16,16,512]{2,1,0:T(8,128)}), f32[16,16,512]{2,1,0:T(8,128)S(1)}, u32[]{:S(2)}, u32[]{:S(2)}) async-start(f32[16,16,512]{2,1,0:T(8,128)} %broadcast_in_dim.59), calls=%async_computation.4 | async-start | bytes 1048576 | tf_op jit(solution)/shard_map/all_to_all | solution.py:21
  237.2 20.7 %all-to-all-start.7 = ((f32[32,1,1]{2,1,0:T(1,128)}), f32[32,1,1]{2,1,0:T(1,128)S(1)}, u32[]{:S(2)}, u32[]{:S(2)}) async-start(f32[32,1,1]{2,1,0:T(1,128)} %broadcast_in_dim.61), calls=%async_computation.7 | async-start | bytes 32768 | tf_op jit(solution)/shard_map/all_to_all | solution.py:21
  259.4 0.6 copy-start.6
  260.0 0.6 copy-start.1
where the time goes:
time: 262 us; the launch traced here: 261 us
  waiting for transfers between devices  162 us (62%)
  starting transfers between devices  68.3 us (26%)
  local copies, waits for them, and re-layouts  16.7 us (6%)
  matrix products  5.5 us (2%)
  other arithmetic  4.07 us (2%)
  between operations  3.88 us (1%)
    all_to_all x6, waiting for transfers between devices, from_everyone(): lax.all_to_all(jnp.broadcast_to(x[None], (peers, *x.shape)), axis, 0, 0,...  106 us
    all_to_all x2, waiting for transfers between devices, sum_at_owner(): tiles = lax.all_to_all(in_blocks(x, dim, peers), axis, 0, 0, tiled=True)  55.8 us
    all_to_all x6, starting transfers between devices, from_everyone(): lax.all_to_all(jnp.broadcast_to(x[None], (peers, *x.shape)), axis, 0, 0,...  53.5 us
    all_to_all x2, starting transfers between devices, sum_at_owner(): tiles = lax.all_to_all(in_blocks(x, dim, peers), axis, 0, 0, tiled=True)  14.9 us
    broadcast_in_dim x6, local copies, waits for them, and re-layouts, from_everyone(): jnp.broadcast_to(x[None], (peers, *x.shape))  6.39 us
    dot_general x2, matrix products, body(): jnp.einsum('tfk,td->fkd', residual, batch, preferred_element_type=jnp.flo...  5.5 us
  transfers between devices with their start and end apart: 8, of which 8 were waited for; matrix products, arithmetic and copies ran while one was open for 3% of the time, Pallas kernels for 0%

commit v1 on v0

v1 whole, which is shorter than its diff:
```python
import functools
import math

import jax
import jax.numpy as jnp
from jax import lax
from jax.experimental import pallas as pl
from jax.experimental.pallas import tpu as pltpu
from jax.sharding import PartitionSpec as P

beta_one = 0.9
beta_two = 0.95
inner_rate = 0.1
adam_eps = 1e-08
decay_rate = 0.1
clip_norm = 0.02
outer_rate = 0.7
outer_momentum = 0.9
mixing = 0.5

NZ, NY, NK = 8, 2, 2
NS = NZ * NY * NK
ROWS = 96
HALF = ROWS // 2
F32, BF16 = jnp.float32, jnp.bfloat16


def kernel(
    n_rep,
    scale,
    grad_scale,
    count_ref,
    first_ref,
    part_ref,
    w_ref,
    m_ref,
    v_ref,
    outer_ref,
    vel_ref,
    new_outer_ref,
    new_inner_ref,
    core_in,
    ring_out,
    ring_in,
    total,
    y_out,
    y_in,
    c_tmp,
    c_out,
    c_in,
    c_full,
    gram,
    n_out,
    n_in,
    rep_out,
    rep_in,
    rep_all,
    core_s,
    core_r,
    ring_s,
    ring_r,
    y_s,
    y_r,
    c_s,
    c_r,
    ag_s,
    ag_r,
    fw_s,
    fw_r,
    n_s,
    n_r,
    rs_s,
    rs_r,
    ra_s,
    ra_r,
):
    rep = lax.axis_index("rep")
    me = lax.axis_index("shard")
    z = me // 4
    y = (me // 2) % 2
    k = me % 2

    def at(zz, yy, kk):
        return (rep, zz * 4 + yy * 2 + kk)

    partner = at(z, y, 1 - k)

    def remote(src, dst, ss, rs, dev):
        return pltpu.make_async_remote_copy(
            src_ref=src,
            dst_ref=dst,
            send_sem=ss,
            recv_sem=rs,
            device_id=dev,
            device_id_type=pl.DeviceIdType.MESH,
        )

    barrier = pltpu.get_barrier_semaphore()

    @pl.loop(1, NS)
    def _(o):
        pl.semaphore_signal(
            barrier, inc=1, device_id=(rep, (me + o) % NS), device_id_type=pl.DeviceIdType.MESH
        )

    @pl.loop(1, n_rep)
    def _(o):
        pl.semaphore_signal(
            barrier, inc=1, device_id=((rep + o) % n_rep, me), device_id_type=pl.DeviceIdType.MESH
        )

    pl.semaphore_wait(barrier, NS - 1 + n_rep - 1)

    def rep_send_copy(s, o):
        to = (rep + o) % n_rep
        return remote(rep_out.at[s, to], rep_in.at[s, o], rs_s.at[s, o], rs_r.at[s, o], (to, me))

    def rep_back_copy(s, o, row):
        to = (rep + o) % n_rep
        return remote(rep_all.at[s, row], rep_all.at[s, row], ra_s.at[s, o], ra_r.at[s, o], (to, me))

    def rep_start(s, value):
        rep_out[s] = value.reshape(n_rep, 1, value.shape[-1])

        @pl.loop(1, n_rep)
        def _(o):
            rep_send_copy(s, o).start()

    def rep_middle(s):
        @pl.loop(1, n_rep)
        def _(o):
            rep_send_copy(s, o).wait_recv()

        acc = rep_out[s, rep]
        for o in range(1, n_rep):
            acc = acc + rep_in[s, o]
        rep_all[s, rep] = acc

        @pl.loop(1, n_rep)
        def _(o):
            rep_back_copy(s, o, rep).start()

    def rep_end(s):
        @pl.loop(1, n_rep)
        def _(o):
            rep_back_copy(s, o, (rep + n_rep - o) % n_rep).wait_recv()

        return rep_all[s].reshape(n_rep, rep_all.shape[-1])

    def core_copy(s):
        return remote(part_ref.at[s, 1 - k], core_in.at[s], core_s.at[s], core_r.at[s], partner)

    def ring_copy(s, d, i):
        zz = (z + 1) % NZ if d == 0 else (z + NZ - 1) % NZ
        return remote(
            ring_out.at[s, d, i], ring_in.at[s, d, i], ring_s.at[s, d, i], ring_r.at[s, d, i], at(zz, y, k)
        )

    def own(s, owner, h):
        rows = pl.ds(HALF * h, HALF)
        return part_ref[s, k, owner, rows, :].astype(F32) + core_in[s, owner, rows, :].astype(F32)

    def ring_send(s, d, long, t):
        hops = 4 if long else 3
        i = t if long else 4 + t
        h = d if long else 1 - d
        owner = (z + hops - t) % NZ if d == 0 else (z + NZ - hops + t) % NZ
        val = own(s, owner, h)
        if t > 0:
            ring_copy(s, d, i - 1).wait_recv()
            val = val + ring_in[s, d, i - 1].astype(F32)
        ring_out[s, d, i] = val.astype(BF16)
        ring_copy(s, d, i).start()

    def ring_step(s, t):
        for long in (True, False):
            if long or t < 3:
                for d in range(2):
                    ring_send(s, d, long, t)

    def y_copy(s):
        return remote(y_out.at[s], y_in.at[s], y_s.at[s], y_r.at[s], at(z, 1 - y, k))

    def y_start(s):
        for h in range(2):
            for i, d in ((3, h), (6, 1 - h)):
                ring_copy(s, d, i).wait_recv()
            total[s, pl.ds(HALF * h, HALF), :] = (
                own(s, z, h) + ring_in[s, h, 3].astype(F32) + ring_in[s, 1 - h, 6].astype(F32)
            )
        y_out[s, pl.ds(0, 32), :] = total[s, pl.ds(32 * (1 - y), 32), :].astype(BF16)
        y_out[s, pl.ds(32, 32), :] = total[s, pl.ds(64, 32), :].astype(BF16)
        y_copy(s).start()

    def c_copy(s):
        return remote(c_out.at[s], c_in.at[s], c_s.at[s], c_r.at[s], partner)

    def ag_copy(s, o, src):
        return remote(
            gram.at[s, src, k], gram.at[s, src, k], ag_s.at[s, o], ag_r.at[s, o], at((z + o) % NZ, y, k)
        )

    def fw_copy(s, o, kk):
        src = (z + NZ - o) % NZ
        return remote(gram.at[s, src, kk], gram.at[s, src, kk], fw_s.at[s, o], fw_r.at[s, o], partner)

    def gather_start(s):
        y_copy(s).wait_recv()
        g = total[s, pl.ds(64, 32), :] + y_in[s, pl.ds(32, 32), :].astype(F32)
        gram[s, z, k] = g.astype(BF16)
        for o in (4, 3, 5, 2, 6, 1, 7):
            ag_copy(s, o, z).start()
        fw_copy(s, 0, k).start()
        c_tmp[s] = total[s, pl.ds(32 * y, 32), :] + y_in[s, pl.ds(0, 32), :].astype(F32)
        c_out[s] = c_tmp[s, pl.ds(16 * (1 - k), 16), :].astype(BF16)
        c_copy(s).start()

    def gather_forward(s):
        for o in (1, 7, 2, 6, 3, 5, 4):
            ag_copy(s, o, (z + NZ - o) % NZ).wait_recv()
            fw_copy(s, o, k).start()

    def gather_end(s):
        c_copy(s).wait_recv()
        c_full[s, k] = c_tmp[s, pl.ds(16 * k, 16), :]
        c_full[s, 1 - k] = c_in[s].astype(F32)
        for o in range(NZ):
            fw_copy(s, o, 1 - k).wait_recv()

    def n_copy(s, o):
        return remote(n_out.at[s], n_in.at[s, o], n_s.at[s, o], n_r.at[s, o], (rep, (me + o) % NS))

    def grad_start(s, w):
        flat = w.reshape(32, 512).astype(BF16)
        prod = jnp.dot(flat, gram[s].reshape(512, 512), preferred_element_type=F32)
        g = (prod * scale - c_full[s].reshape(32, 512)) * grad_scale
        n_out[s] = jnp.broadcast_to(jnp.sum(jnp.sum(g * g, axis=0, keepdims=True), axis=1, keepdims=True), (1, 128))

        @pl.loop(1, NS)
        def _(o):
            n_copy(s, o).start()

        return g.reshape(2, 16, 512)

    def clip_factor(s):
        @pl.loop(1, NS)
        def _(o):
            n_copy(s, o).wait_recv()

        acc = n_out[s]
        for o in range(1, NS):
            acc = acc + n_in[s, o]
        f = jnp.minimum(1.0, clip_norm / (jnp.sqrt(acc) + 1e-06))
        return f[:, :1].reshape(1, 1, 1)

    def adam(s, w, m, v, clipped):
        count = jnp.full((1, 8, 128), count_ref[0].astype(F32) + s, F32)
        one = (1.0 - jnp.exp(count * math.log(beta_one)))[:, :1, :1]
        two = (1.0 - jnp.exp(count * math.log(beta_two)))[:, :1, :1]
        m = beta_one * m + (1.0 - beta_one) * clipped
        v = beta_two * v + (1.0 - beta_two) * clipped * clipped
        update = m / one / (jnp.sqrt(v / two) + adam_eps)
        return w - inner_rate * (update + decay_rate * w), m, v

    lead = first_ref[0] == 0

    def outer_step(theta, speed, weight_sum):
        delta = theta - weight_sum * (1.0 / n_rep)
        speed = outer_momentum * speed + delta
        return theta - outer_rate * (outer_momentum * speed + delta)

    w, m, v = w_ref[...], m_ref[...], v_ref[...]
    core_copy(0).start()
    rep_start(0, jnp.where(lead, w[0], w[1]))
    core_copy(1).start()
    core_copy(0).wait_recv()
    for t in range(4):
        ring_step(0, t)
    rep_middle(0)
    y_start(0)
    core_copy(1).wait_recv()
    ring_step(1, 0)
    ring_step(1, 1)
    gather_start(0)
    ring_step(1, 2)
    gather_forward(0)
    ring_step(1, 3)
    gather_end(0)
    g = grad_start(0, w)
    y_start(1)
    clipped = g * clip_factor(0)
    w, m, v = adam(0, w, m, v, clipped)
    rep_start(1, jnp.where(lead, w[1], w[0]))
    theta0 = outer_step(
        jnp.where(lead, outer_ref[0], outer_ref[1]), jnp.where(lead, vel_ref[0], vel_ref[1]), rep_end(0)
    )
    a = jnp.where(lead, mixing * theta0 + (1.0 - mixing) * w[0], w[0])
    b = jnp.where(lead, w[1], mixing * theta0 + (1.0 - mixing) * w[1])
    w = jnp.stack([a, b])
    gather_start(1)
    gather_forward(1)
    gather_end(1)
    g = grad_start(1, w)
    rep_middle(1)
    clipped = g * clip_factor(1)
    w, m, v = adam(1, w, m, v, clipped)
    theta1 = outer_step(
        jnp.where(lead, outer_ref[1], outer_ref[0]), jnp.where(lead, vel_ref[1], vel_ref[0]), rep_end(1)
    )
    new_inner_ref[0] = jnp.where(lead, w[0], mixing * theta1 + (1.0 - mixing) * w[0])
    new_inner_ref[1] = jnp.where(lead, mixing * theta1 + (1.0 - mixing) * w[1], w[1])
    new_outer_ref[0] = jnp.where(lead, theta0, theta1)
    new_outer_ref[1] = jnp.where(lead, theta1, theta0)

    for s in range(2):
        core_copy(s).wait_send()
        y_copy(s).wait_send()
        c_copy(s).wait_send()
        for d in range(2):
            for i in range(7):
                ring_copy(s, d, i).wait_send()
        for o in range(1, NZ):
            ag_copy(s, o, z).wait_send()
        for o in range(NZ):
            fw_copy(s, o, k).wait_send()

        @pl.loop(1, NS)
        def _(o):
            n_copy(s, o).wait_send()

        @pl.loop(1, n_rep)
        def _(o):
            rep_send_copy(s, o).wait_send()
            rep_back_copy(s, o, rep).wait_send()


def body(
    inner_weights,
    first_moment,
    second_moment,
    outer_weights,
    outer_velocity,
    tokens,
    targets,
    step_count,
    first_fragment,
):
    n_rep = lax.axis_size("rep")
    tok_dev, width = tokens.shape[2:]
    scale = 1.0 / math.sqrt(width)
    grad_scale = scale / (tok_dev * NS)
    parts = []
    for s in range(2):
        x = tokens[0, s]
        gram = jnp.einsum("td,te->de", x, x, preferred_element_type=F32).astype(BF16)
        cross = jnp.einsum("tfk,td->fkd", targets[0, s], x, preferred_element_type=F32).astype(BF16)
        gram = jnp.moveaxis(gram.reshape(NZ, NK, 32, width), 1, 0)
        parts.append(jnp.concatenate([cross.reshape(2, NZ, 64, width), gram], axis=2))
    part = jnp.stack(parts)
    vmem = pl.BlockSpec(memory_space=pltpu.VMEM)
    smem = pl.BlockSpec(memory_space=pltpu.SMEM)
    dma = pltpu.SemaphoreType.DMA
    D = width
    new_outer, new_inner = pl.pallas_call(
        functools.partial(kernel, n_rep, scale, grad_scale),
        name="window",
        out_shape=(
            jax.ShapeDtypeStruct((2, 16, D), F32),
            jax.ShapeDtypeStruct((2, 16, D), F32),
        ),
        in_specs=[smem, smem] + [vmem] * 6,
        out_specs=(vmem, vmem),
        scratch_shapes=[
            pltpu.VMEM((2, NZ, ROWS, D), BF16),
            pltpu.VMEM((2, 2, 7, HALF, D), BF16),
            pltpu.VMEM((2, 2, 7, HALF, D), BF16),
            pltpu.VMEM((2, ROWS, D), F32),
            pltpu.VMEM((2, 64, D), BF16),
            pltpu.VMEM((2, 64, D), BF16),
            pltpu.VMEM((2, 32, D), F32),
            pltpu.VMEM((2, 16, D), BF16),
            pltpu.VMEM((2, 16, D), BF16),
            pltpu.VMEM((2, 2, 16, D), F32),
            pltpu.VMEM((2, NZ, NK, 32, D), BF16),
            pltpu.VMEM((2, 1, 128), F32),
            pltpu.VMEM((2, NS, 1, 128), F32),
            pltpu.VMEM((2, n_rep, 1, D), F32),
            pltpu.VMEM((2, n_rep, 1, D), F32),
            pltpu.VMEM((2, n_rep, 1, D), F32),
            dma((2,)),
            dma((2,)),
            dma((2, 2, 7)),
            dma((2, 2, 7)),
            dma((2,)),
            dma((2,)),
            dma((2,)),
            dma((2,)),
            dma((2, NZ)),
            dma((2, NZ)),
            dma((2, NZ)),
            dma((2, NZ)),
            dma((2, NS)),
            dma((2, NS)),
            dma((2, n_rep)),
            dma((2, n_rep)),
            dma((2, n_rep)),
            dma((2, n_rep)),
        ],
        compiler_params=pltpu.CompilerParams(collective_id=0, has_side_effects=True),
    )(
        step_count,
        first_fragment,
        part,
        inner_weights[0],
        first_moment[0],
        second_moment[0],
        outer_weights,
        outer_velocity,
    )
    return new_outer, new_inner[None]


def solution(mesh):
    in_specs = (
        P("rep", None, "shard", None),
        P("rep", None, "shard", None),
        P("rep", None, "shard", None),
        P(None, "shard", None),
        P(None, "shard", None),
        P("rep", None, "shard", None),
        P("rep", None, "shard", None, None),
        P(),
        P(),
    )
    out_specs = (P(None, "shard", None), P("rep", None, "shard", None))
    return jax.shard_map(body, mesh=mesh, in_specs=in_specs, out_specs=out_specs, check_vma=False)
```

time: 262 us -> 98.1 us (0.37)
  waiting for transfers between devices: 162 us -> 0 us
  Pallas kernels: 0 us -> 79.9 us
  starting transfers between devices: 68.3 us -> 0 us
  local copies, waits for them, and re-layouts: 16.7 us -> 9.26 us
    all_to_all x8 -> x0, waiting for transfers between devices: 162 us -> none  [the longest x6 106 us: from_everyone(): lax.all_to_all(jnp.broadcast_to(x[None], (peers, *x.shape)), axis, 0, 0,...]
    pallas_call x0 -> x1, Pallas kernels: none -> 79.9 us  [body(): pl.pallas_call(functools.partial(kernel, n_rep, scale, grad_scale), name=...]
    all_to_all x8 -> x0, starting transfers between devices: 68.3 us -> none  [the longest x6 53.5 us: from_everyone(): lax.all_to_all(jnp.broadcast_to(x[None], (peers, *x.shape)), axis, 0, 0,...]
    broadcast_in_dim x6 -> x0, local copies, waits for them, and re-layouts: 6.39 us -> none  [from_everyone(): jnp.broadcast_to(x[None], (peers, *x.shape))]
    reduce_sum x8 -> x0, other arithmetic: 2.96 us -> none  [the longest x4 1.34 us: of_everyone(): return jnp.sum(everything, axis=0)]
    unnamed x17 -> x8, local copies, waits for them, and re-layouts: 4.58 us -> 6.5 us
    dot_general x2 -> x4, matrix products: 5.5 us -> 4.35 us  [the longest x2 3.42 us: body(): jnp.einsum('tfk,td->fkd', targets[0, s], x, preferred_element_type=F32)]
  transfers between devices with their start and end apart: 8 -> 0, of which waited for: 8 -> 0; matrix products, arithmetic and copies ran while one was open for 3% -> 0% of each run, Pallas kernels for 0% -> 0%
where the time goes in v1:
time: 98.1 us; the launch traced here: 97.8 us
  Pallas kernels  79.9 us (81%)
  local copies, waits for them, and re-layouts  9.26 us (9%)
  matrix products  4.35 us (4%)
  other arithmetic  2.23 us (2%)
  between operations  2.02 us (2%)
    pallas_call x1, Pallas kernels, body(): pl.pallas_call(functools.partial(kernel, n_rep, scale, grad_scale), name=...  79.9 us
    unnamed x8, local copies, waits for them, and re-layouts  6.5 us
    dot_general x2, matrix products, body(): jnp.einsum('tfk,td->fkd', targets[0, s], x, preferred_element_type=F32)  3.42 us
    slice x1, local copies, waits for them, and re-layouts, body(): targets[0, s]  2.68 us
    another operation x2, other arithmetic, body(): part = jnp.stack(parts)  2.23 us

profile of v1, /device:TPU:1, one launch (start us, length us, event | category | flops | bytes accessed | tf_op | source)
XLA Modules:
  0.0 97.8 jit_solution(1630654646818240741)
XLA Ops:
  0.6 2.7 %fusion.10 = (bf16[1,1,512,2,512]{4,3,2,1,0:T(2,128)(2,1)S(1)}, bf16[1,1,512,2,512]{4,3,2,1,0:T(2,128)(2,1)S(1)}) fusion(bf16[1,2,512,2,512]{4,3,2,1,0:T(2,128)(2,1)} %param.15), kind=kLoop, calls=%fused_computation.19 | loop fusion | bytes 4194304 | tf_op jit(solution)/shard_map/slice | solution.py:356
  3.3 1.5 %copy.18 = bf16[1,1,512,2,512]{2,4,3,1,0:T(8,128)(2,1)S(1)} copy(bf16[1,1,512,2,512]{4,3,2,1,0:T(2,128)(2,1)S(1)} %get-tuple-element.7) | data formatting | bytes 2097152
  4.8 2.7 %convolution_convert_fusion = bf16[2,512,512]{2,1,0:T(8,128)(2,1)} fusion(bf16[1,1,512,2,512]{2,4,3,1,0:T(8,128)(2,1)S(1)} %copy.18, bf16[1,2,512,512]{3,2,1,0:T(8,128)(2,1)} %param.14), kind=kOutput, calls=%fused_computation.3 | convolution fusion | flops 537395200 | bytes 2621440 | tf_op jit(solution)/shard_map/tfk,td->fkd/dot_general | solution.py:356
  7.5 0.0 copy-start.1
  7.5 1.4 %copy.17 = bf16[1,1,512,2,512]{2,4,3,1,0:T(8,128)(2,1)S(1)} copy(bf16[1,1,512,2,512]{4,3,2,1,0:T(2,128)(2,1)S(1)} %get-tuple-element.6) | data formatting | bytes 2097152
  9.0 0.0 copy-done.1
  9.0 0.7 convolution_convert_fusion.1
  9.7 0.5 convolution_convert_fusion.2
  10.1 0.0 copy-start
  10.2 0.5 convolution_convert_fusion.3
  10.7 0.6 copy-done
  11.4 0.3 maximum_bitcast_fusion
  11.7 1.9 %pad_maximum_fusion.part_ref = bf16[2,2,8,96,512]{4,3,2,1,0:T(8,128)(2,1)} fusion(bf16[1,2,8,96,512]{4,3,2,1,0:T(8,128)(2,1)S(1)} %get-tuple-element.9, bf16[1,2,8,96,512]{4,3,2,1,0:T(8,128)(2,1)S(1)} %get-tuple-element.8), kind=kLoop, calls=%fused_computation | loop fusion | flops 1572864 | bytes 6291456 | tf_op jit(solution)/shard_map/stack | solution.py:359
  14.9 79.9 %window.1 = (f32[2,16,512]{2,1,0:T(8,128)}, f32[2,16,512]{2,1,0:T(8,128)}) custom-call(s32[1]{0:T(128)S(6)} %copy.25.count_ref, s32[1]{0:T(128)S(6)} %copy.26.first_ref, bf16[2,2,8,96,512]{4,3,2,1,0:T(8,128)(2,1)} %pad_maximum_fusion.part_ref, f32[2,16,512]{2,1,0:T(8,128)} %bitcast.44, f32[2,16,512]{2,1,0:T(8,128)} %bitcast.45, f32[2,16,512]{2,1,0:T(8,128)} %bitcast.46, ...), custom_call_target="tpu_custom_call" | custom-call | tf_op jit(solution)/shard_map/window/pallas_call | solution.py:364
  94.8 1.5 %copy.27 = f32[2,16,512]{2,1,0:T(8,128)} copy(f32[2,16,512]{2,1,0:T(8,128)} %get-tuple-element.12) | data formatting | bytes 131072
  96.3 1.5 %copy.28 = f32[1,2,16,512]{3,2,1,0:T(8,128)} copy(f32[1,2,16,512]{3,2,1,0:T(8,128)} %bitcast.47) | data formatting | bytes 131072
  (2 shorter events, 0.1 us)
Async XLA Ops:
  7.5 1.5 %copy-start.1 = (bf16[1,2,512,512]{3,2,1,0:T(8,128)(2,1)S(1)}, bf16[1,2,512,512]{3,2,1,0:T(8,128)(2,1)}, u32[]{:S(2)}) copy-start(bf16[1,2,512,512]{3,2,1,0:T(8,128)(2,1)} %param.14) | copy-start | bytes 3145732
  10.1 1.2 %copy-start = (bf16[2,512,512]{2,1,0:T(8,128)(2,1)S(1)}, bf16[2,512,512]{2,1,0:T(8,128)(2,1)}, u32[]{:S(2)}) copy-start(bf16[2,512,512]{2,1,0:T(8,128)(2,1)} %convolution_convert_fusion) | copy-start | bytes 3145732

commit v2 on v0

v2 whole, which is shorter than its diff:
```python
import functools
import math

import jax
import jax.numpy as jnp
from jax import lax
from jax.experimental import pallas as pl
from jax.experimental.pallas import tpu as pltpu
from jax.sharding import PartitionSpec as P

beta_one = 0.9
beta_two = 0.95
inner_rate = 0.1
adam_eps = 1e-08
decay_rate = 0.1
clip_norm = 0.02
outer_rate = 0.7
outer_momentum = 0.9
mixing = 0.5

NZ, NY, NK = 8, 2, 2
NS = NZ * NY * NK
MESH = pl.DeviceIdType.MESH
F32, BF16 = jnp.float32, jnp.bfloat16


class Ring:
    def __init__(self, dev, mine, other, out, got, ss, rs, half, sub):
        self.dev, self.mine, self.other = dev, mine, other
        self.out, self.got, self.ss, self.rs = out, got, ss, rs
        self.half, self.sub = half, sub

    def copy(self, d, i, u):
        z, y, k, at, remote = self.dev
        zz = (z + 1) % NZ if d == 0 else (z + NZ - 1) % NZ
        rows = pl.ds(u * self.sub, self.sub)
        return remote(
            self.out.at[d, i, rows], self.got.at[d, i, rows], self.ss.at[d, i, u], self.rs.at[d, i, u], at(zz, y, k)
        )

    def own(self, owner, h, u):
        k = self.dev[2]
        rows = pl.ds(self.half * h + u * self.sub, self.sub)
        return self.mine[k, owner, rows, :].astype(F32) + self.other[owner, rows, :].astype(F32)

    def arrived(self, d, i, u):
        self.copy(d, i, u).wait_recv()
        return self.got[d, i, pl.ds(u * self.sub, self.sub), :].astype(F32)

    def step(self, t):
        z = self.dev[0]
        for long in (True, False):
            if not long and t == 3:
                continue
            hops = 4 if long else 3
            i = t if long else 4 + t
            for u in range(self.half // self.sub):
                for d in range(2):
                    h = d if long else 1 - d
                    owner = (z + hops - t) % NZ if d == 0 else (z + NZ - hops + t) % NZ
                    val = self.own(owner, h, u)
                    if t > 0:
                        val = val + self.arrived(d, i - 1, u)
                    self.out[d, i, pl.ds(u * self.sub, self.sub), :] = val.astype(BF16)
                    self.copy(d, i, u).start()

    def finish(self, total):
        z = self.dev[0]
        for u in range(self.half // self.sub):
            for h in range(2):
                val = self.own(z, h, u) + self.arrived(1 - h, 6, u) + self.arrived(h, 3, u)
                total[pl.ds(self.half * h + u * self.sub, self.sub), :] = val

    def drain(self):
        for d in range(2):
            for i in range(7):
                for u in range(self.half // self.sub):
                    self.copy(d, i, u).wait_send()


def kernel(n_rep, scale, grad_scale, count_ref, first_ref, x_hbm, t_hbm, w_ref, m_ref, v_ref, outer_ref, vel_ref, out_ref, *scratch):
    names, shapes = zip(*scratch_of(n_rep))
    r = dict(zip(names, scratch, strict=True))
    rep = lax.axis_index("rep")
    me = lax.axis_index("shard")
    z = me // 4
    y = (me // 2) % 2
    k = me % 2
    q = z * 2 + k

    def at(zz, yy, kk):
        return (rep, zz * 4 + yy * 2 + kk)

    def plane(qq):
        return at(qq // 2, y, qq % 2)

    partner = at(z, y, 1 - k)
    across = at(z, 1 - y, k)

    def remote(src, dst, ss, rs, dev):
        return pltpu.make_async_remote_copy(
            src_ref=src, dst_ref=dst, send_sem=ss, recv_sem=rs, device_id=dev, device_id_type=MESH
        )

    barrier = pltpu.get_barrier_semaphore()

    @pl.loop(1, NS)
    def _(o):
        pl.semaphore_signal(barrier, inc=1, device_id=(rep, (me + o) % NS), device_id_type=MESH)

    @pl.loop(1, n_rep)
    def _(o):
        pl.semaphore_signal(barrier, inc=1, device_id=((rep + o) % n_rep, me), device_id_type=MESH)

    def load(s):
        return (
            pltpu.make_async_copy(x_hbm.at[s], r["x"].at[s], r["load"].at[s, 0]),
            pltpu.make_async_copy(t_hbm.at[s], r["t"].at[s], r["load"].at[s, 1]),
        )

    for s in range(2):
        for c in load(s):
            c.start()

    rep_out, rep_in, rep_all = r["rep_out"], r["rep_in"], r["rep_all"]

    def rep_send_copy(s, o):
        to = (rep + o) % n_rep
        return remote(rep_out.at[s, to], rep_in.at[s, o], r["rs_s"].at[s, o], r["rs_r"].at[s, o], (to, me))

    def rep_back_copy(s, o, row):
        to = (rep + o) % n_rep
        return remote(rep_all.at[s, row], rep_all.at[s, row], r["ra_s"].at[s, o], r["ra_r"].at[s, o], (to, me))

    def rep_start(s, value):
        rep_out[s] = value.reshape(n_rep, 1, value.shape[-1])

        @pl.loop(1, n_rep)
        def _(o):
            rep_send_copy(s, o).start()

    def rep_middle(s):
        @pl.loop(1, n_rep)
        def _(o):
            rep_send_copy(s, o).wait_recv()

        acc = rep_out[s, rep]
        for o in range(1, n_rep):
            acc = acc + rep_in[s, o]
        rep_all[s, rep] = acc

        @pl.loop(1, n_rep)
        def _(o):
            rep_back_copy(s, o, rep).start()

    def rep_end(s):
        @pl.loop(1, n_rep)
        def _(o):
            rep_back_copy(s, o, (rep + n_rep - o) % n_rep).wait_recv()

        return rep_all[s].reshape(n_rep, rep_all.shape[-1])

    def core_a():
        return remote(r["pa"].at[1 - k], r["ca"], r["core_s"].at[0], r["core_r"].at[0], partner)

    def core_b():
        return remote(r["pb"].at[1 - k], r["cb"], r["core_s"].at[1], r["core_r"].at[1], partner)

    dev = (z, y, k, at, remote)
    ring_a = Ring(dev, r["pa"], r["ca"], r["ra_out"], r["ra_in"], r["ring_a_s"], r["ring_a_r"], 64, SUB_A)
    ring_b = Ring(dev, r["pb"], r["cb"], r["rb_out"], r["rb_in"], r["ring_b_s"], r["ring_b_r"], 32, SUB_B)

    def tdot(a, b):
        return lax.dot_general(a, b, (((0,), (0,)), ((), ())), preferred_element_type=F32)

    def gram_rows(s, first_row):
        x = r["x"][s]
        g = tdot(x, x).astype(BF16).reshape(NZ, NK, 32, 512)
        for kk in range(NK):
            r["pa"][kk, :, pl.ds(first_row, 32), :] = g[:, kk]

    for c in load(0):
        c.wait()
    gram_rows(0, 64)
    flat = r["t"][0].reshape(512, 1024)
    for kk in range(NK):
        ct = tdot(r["x"][0], flat[:, 512 * kk : 512 * kk + 512])
        r["pa"][kk, :, pl.ds(0, 64), :] = ct.astype(BF16).reshape(NZ, 64, 512)
    for c in load(1):
        c.wait()
    gram_rows(1, 96)
    w, m, v = w_ref[...], m_ref[...], v_ref[...]
    r["wb"][...] = w.astype(BF16)
    r["wall"][z, k] = r["wb"][k]

    pl.semaphore_wait(barrier, NS - 1 + n_rep - 1)
    core_a().start()

    def w_swap():
        return remote(r["wb"].at[1 - k], r["wall"].at[z, k], r["wsw_s"], r["wsw_r"], partner)

    def w_copy(d, t, block):
        zz = (z + 1) % NZ if d == 0 else (z + NZ - 1) % NZ
        return remote(r["wall"].at[block], r["wall"].at[block], r["w_s"].at[d, t], r["w_r"].at[d, t], at(zz, y, k))

    def w_step(t):
        if t == 0:
            remote(r["wb"].at[k], r["wall"].at[z, 1 - k], r["wsw_s"], r["wsw_r"], partner).wait_recv()
        for d in range(2 if t < 3 else 1):
            block = (z + NZ - t) % NZ if d == 0 else (z + t) % NZ
            if t > 0:
                w_copy(d, t - 1, block).wait_recv()
            w_copy(d, t, block).start()

    w_swap().start()
    lead = first_ref[0] == 0
    rep_start(0, jnp.where(lead, w[0], w[1]))

    flat = r["t"][1].reshape(512, 1024)
    for kk in range(NK):
        c1 = tdot(flat[:, 512 * kk : 512 * kk + 512], r["x"][1])
        r["pb"][kk] = c1.astype(BF16).reshape(NZ, 64, 512)
    core_b().start()
    row = lax.broadcasted_iota(jnp.int32, (512, 256), 0)
    col = lax.broadcasted_iota(jnp.int32, (512, 256), 1)
    place = jnp.where((row // 64 == col // 32) & (row % 32 == col % 32), (row // 32) % 2, 2)
    pick_mine = jnp.where(place == y, 1.0, 0.0).astype(BF16)
    pick_other = jnp.where(place == 1 - y, 1.0, 0.0).astype(BF16)

    core_a().wait_recv()
    for t in range(4):
        ring_a.step(t)
        w_step(t)

    def y_copy(i):
        name = ("yc", "yg0", "yg1")[i]
        return remote(r[name + "_out"], r[name + "_in"], r["y_s"].at[i], r["y_r"].at[i], across)

    ring_a.finish(r["ta"])
    hi = r["ta"][pl.ds(0, 64), :].astype(BF16)
    lo = (r["ta"][pl.ds(0, 64), :] - hi.astype(F32)).astype(BF16)
    r["yc_out"][...] = jnp.dot(hi, pick_other, preferred_element_type=F32).astype(BF16)
    y_copy(0).start()
    r["yg0_out"][...] = r["ta"][pl.ds(64, 32), :].astype(BF16)
    y_copy(1).start()
    r["yg1_out"][...] = r["ta"][pl.ds(96, 32), :].astype(BF16)
    y_copy(2).start()
    rep_middle(0)
    core_b().wait_recv()
    ring_b.step(0)
    cross = jnp.dot(hi, pick_mine, preferred_element_type=F32) + jnp.dot(lo, pick_mine, preferred_element_type=F32)
    w_copy(0, 3, (z + NZ - 4) % NZ).wait_recv()
    w_copy(1, 2, (z + 3) % NZ).wait_recv()

    def g0_swap(kk):
        return remote(r["gcol"].at[kk], r["gcol"].at[kk], r["gsw_s"], r["gsw_r"], partner)

    y_copy(0).wait_recv()
    cross = cross + r["yc_in"][...].astype(F32)
    y_copy(1).wait_recv()
    r["gcol"][k] = (r["ta"][pl.ds(64, 32), :] + r["yg0_in"][...].astype(F32)).astype(BF16)
    g0_swap(k).start()

    def ag_copy(o, src):
        return remote(
            r["gram"].at[src, k], r["gram"].at[src, k], r["ag_s"].at[o], r["ag_r"].at[o], at((z + o) % NZ, y, k)
        )

    def fw_copy(o, kk):
        src = (z + NZ - o) % NZ
        return remote(r["gram"].at[src, kk], r["gram"].at[src, kk], r["fw_s"].at[o], r["fw_r"].at[o], partner)

    y_copy(2).wait_recv()
    r["gram"][z, k] = (r["ta"][pl.ds(96, 32), :] + r["yg1_in"][...].astype(F32)).astype(BF16)

    def a_copy(o):
        to = (q + o) % 16
        return remote(r["gout"].at[to], r["gin"].at[k, z], r["a_s"].at[o], r["a_r"].at[o], plane(to))

    def a_from(o):
        src = (q + 16 - o) % 16
        return remote(r["gout"].at[q], r["gin"].at[src % 2, src // 2], r["a_s"].at[o], r["a_r"].at[o], plane(src))

    def n_copy(s, o):
        return remote(r["n_out"].at[s], r["n_in"].at[s, o], r["n_s"].at[s, o], r["n_r"].at[s, o], (rep, (me + o) % NS))

    def norm_start(s, g):
        total = jnp.sum(jnp.sum(g * g, axis=0, keepdims=True), axis=1, keepdims=True)
        r["n_out"][s] = jnp.broadcast_to(total, (1, 128))

        @pl.loop(1, NS)
        def _(o):
            n_copy(s, o).start()

    def clip_factor(s):
        @pl.loop(1, NS)
        def _(o):
            n_copy(s, o).wait_recv()

        acc = r["n_out"][s]
        for o in range(1, NS):
            acc = acc + r["n_in"][s, o]
        f = jnp.minimum(1.0, clip_norm / (jnp.sqrt(acc) + 1e-06))
        return f[:, :1].reshape(1, 1, 1)

    def ndot(a, b):
        return lax.dot_general(a, b, (((1,), (1,)), ((), ())), preferred_element_type=F32)

    g0_swap(1 - k).wait_recv()
    gt = ndot(r["gcol"][...].reshape(64, 512), r["wall"][...].reshape(256, 512))
    gt = (gt * scale - cross) * grad_scale
    norm_start(0, gt)
    r["gout"][...] = gt.T.astype(BF16).reshape(16, 16, 64)
    r["gin"][k, z] = r["gout"][q]

    @pl.loop(1, 16)
    def _(o):
        a_copy(o).start()

    for o in (4, 3, 5, 2, 6, 1, 7):
        ag_copy(o, z).start()
    fw_copy(0, k).start()
    ring_b.step(1)
    ring_b.step(2)
    for o in (1, 7, 2, 6):
        ag_copy(o, (z + NZ - o) % NZ).wait_recv()
        fw_copy(o, k).start()
    ring_b.step(3)
    for o in (3, 5, 4):
        ag_copy(o, (z + NZ - o) % NZ).wait_recv()
        fw_copy(o, k).start()

    ring_b.finish(r["tb"])
    peers = ((0, 1 - k), (1, k), (1, 1 - k))

    def c_copy(i):
        dy, kk = peers[i]
        yy = y if dy == 0 else 1 - y
        return remote(r["c_out"].at[i], r["c_in"].at[i], r["c_s"].at[i], r["c_r"].at[i], at(z, yy, kk))

    for i in (2, 1, 0):
        dy, kk = peers[i]
        yy = y if dy == 0 else 1 - y
        r["c_out"][i] = r["tb"][pl.ds(yy * 32 + kk * 16, 16), :].astype(BF16)
        c_copy(i).start()

    def adam(s, w, m, v, clipped):
        count = jnp.full((1, 8, 128), count_ref[0].astype(F32) + s, F32)
        one = (1.0 - jnp.exp(count * math.log(beta_one)))[:, :1, :1]
        two = (1.0 - jnp.exp(count * math.log(beta_two)))[:, :1, :1]
        m = beta_one * m + (1.0 - beta_one) * clipped
        v = beta_two * v + (1.0 - beta_two) * clipped * clipped
        update = m / one / (jnp.sqrt(v / two) + adam_eps)
        return w - inner_rate * (update + decay_rate * w), m, v

    def outer_step(theta, speed, weight_sum):
        delta = theta - weight_sum * (1.0 / n_rep)
        speed = outer_momentum * speed + delta
        return theta - outer_rate * (outer_momentum * speed + delta)

    theta0 = outer_step(
        jnp.where(lead, outer_ref[0], outer_ref[1]), jnp.where(lead, vel_ref[0], vel_ref[1]), rep_end(0)
    )

    @pl.loop(1, 16)
    def _(o):
        a_from(o).wait_recv()

    for zz in range(NZ):
        for f in range(2):
            r["g0"][f, :, 64 * zz : 64 * zz + 64] = r["gin"][f, zz].astype(F32)
    clipped = r["g0"][...] * clip_factor(0)
    w, m, v = adam(0, w, m, v, clipped)
    rep_start(1, jnp.where(lead, w[1], w[0]))
    a = jnp.where(lead, mixing * theta0 + (1.0 - mixing) * w[0], w[0])
    b = jnp.where(lead, w[1], mixing * theta0 + (1.0 - mixing) * w[1])
    w = jnp.stack([a, b])
    for o in range(NZ):
        fw_copy(o, 1 - k).wait_recv()
    prod = jnp.dot(w.reshape(32, 512).astype(BF16), r["gram"][...].reshape(512, 512), preferred_element_type=F32)
    for i in range(3):
        c_copy(i).wait_recv()
    r["c1"][k] = r["tb"][pl.ds(y * 32 + k * 16, 16), :] + r["c_in"][1].astype(F32)
    r["c1"][1 - k] = r["c_in"][0].astype(F32) + r["c_in"][2].astype(F32)
    g = (prod * scale - r["c1"][...].reshape(32, 512)) * grad_scale
    norm_start(1, g)
    rep_middle(1)
    clipped = g.reshape(2, 16, 512) * clip_factor(1)
    w, m, v = adam(1, w, m, v, clipped)
    theta1 = outer_step(
        jnp.where(lead, outer_ref[1], outer_ref[0]), jnp.where(lead, vel_ref[1], vel_ref[0]), rep_end(1)
    )
    out_ref[0] = jnp.where(lead, theta0, theta1)
    out_ref[1] = jnp.where(lead, theta1, theta0)
    out_ref[2] = jnp.where(lead, w[0], mixing * theta1 + (1.0 - mixing) * w[0])
    out_ref[3] = jnp.where(lead, mixing * theta1 + (1.0 - mixing) * w[1], w[1])

    core_a().wait_send()
    core_b().wait_send()
    ring_a.drain()
    ring_b.drain()
    w_swap().wait_send()
    for t in range(4):
        for d in range(2 if t < 3 else 1):
            w_copy(d, t, (z + NZ - t) % NZ if d == 0 else (z + t) % NZ).wait_send()
    for i in range(3):
        y_copy(i).wait_send()
        c_copy(i).wait_send()
    g0_swap(k).wait_send()
    for o in range(1, NZ):
        ag_copy(o, z).wait_send()
    for o in range(NZ):
        fw_copy(o, k).wait_send()

    @pl.loop(1, 16)
    def _(o):
        a_copy(o).wait_send()

    for s in range(2):

        @pl.loop(1, NS)
        def _(o):
            n_copy(s, o).wait_send()

        @pl.loop(1, n_rep)
        def _(o):
            rep_send_copy(s, o).wait_send()
            rep_back_copy(s, o, rep).wait_send()


SUB_A, SUB_B = 32, 32


def scratch_of(n_rep):
    vmem, dma = pltpu.VMEM, pltpu.SemaphoreType.DMA
    D = 512
    return (
        ("x", vmem((2, 512, D), BF16)),
        ("t", vmem((2, 512, 2, D), BF16)),
        ("pa", vmem((NK, NZ, 128, D), BF16)),
        ("pb", vmem((NK, NZ, 64, D), BF16)),
        ("ca", vmem((NZ, 128, D), BF16)),
        ("cb", vmem((NZ, 64, D), BF16)),
        ("ra_out", vmem((2, 7, 64, D), BF16)),
        ("ra_in", vmem((2, 7, 64, D), BF16)),
        ("rb_out", vmem((2, 7, 32, D), BF16)),
        ("rb_in", vmem((2, 7, 32, D), BF16)),
        ("ta", vmem((128, D), F32)),
        ("tb", vmem((64, D), F32)),
        ("wb", vmem((2, 16, D), BF16)),
        ("wall", vmem((NZ, NK, 16, D), BF16)),
        ("yc_out", vmem((64, 256), BF16)),
        ("yc_in", vmem((64, 256), BF16)),
        ("yg0_out", vmem((32, D), BF16)),
        ("yg0_in", vmem((32, D), BF16)),
        ("yg1_out", vmem((32, D), BF16)),
        ("yg1_in", vmem((32, D), BF16)),
        ("gcol", vmem((NK, 32, D), BF16)),
        ("gram", vmem((NZ, NK, 32, D), BF16)),
        ("gout", vmem((16, 16, 64), BF16)),
        ("gin", vmem((2, NZ, 16, 64), BF16)),
        ("g0", vmem((2, 16, D), F32)),
        ("c_out", vmem((3, 16, D), BF16)),
        ("c_in", vmem((3, 16, D), BF16)),
        ("c1", vmem((2, 16, D), F32)),
        ("n_out", vmem((2, 1, 128), F32)),
        ("n_in", vmem((2, NS, 1, 128), F32)),
        ("rep_out", vmem((2, n_rep, 1, D), F32)),
        ("rep_in", vmem((2, n_rep, 1, D), F32)),
        ("rep_all", vmem((2, n_rep, 1, D), F32)),
        ("load", dma((2, 2))),
        ("core_s", dma((2,))),
        ("core_r", dma((2,))),
        ("ring_a_s", dma((2, 7, 64 // SUB_A))),
        ("ring_a_r", dma((2, 7, 64 // SUB_A))),
        ("ring_b_s", dma((2, 7, 32 // SUB_B))),
        ("ring_b_r", dma((2, 7, 32 // SUB_B))),
        ("wsw_s", dma),
        ("wsw_r", dma),
        ("w_s", dma((2, 4))),
        ("w_r", dma((2, 4))),
        ("y_s", dma((3,))),
        ("y_r", dma((3,))),
        ("gsw_s", dma),
        ("gsw_r", dma),
        ("ag_s", dma((NZ,))),
        ("ag_r", dma((NZ,))),
        ("fw_s", dma((NZ,))),
        ("fw_r", dma((NZ,))),
        ("a_s", dma((16,))),
        ("a_r", dma((16,))),
        ("c_s", dma((3,))),
        ("c_r", dma((3,))),
        ("n_s", dma((2, NS))),
        ("n_r", dma((2, NS))),
        ("rs_s", dma((2, n_rep))),
        ("rs_r", dma((2, n_rep))),
        ("ra_s", dma((2, n_rep))),
        ("ra_r", dma((2, n_rep))),
    )


def body(
    inner_weights,
    first_moment,
    second_moment,
    outer_weights,
    outer_velocity,
    tokens,
    targets,
    step_count,
    first_fragment,
):
    n_rep = lax.axis_size("rep")
    tok_dev, width = tokens.shape[2:]
    scale = 1.0 / math.sqrt(width)
    grad_scale = scale / (tok_dev * NS)
    vmem = pl.BlockSpec(memory_space=pltpu.VMEM)
    smem = pl.BlockSpec(memory_space=pltpu.SMEM)
    anywhere = pl.BlockSpec(memory_space=pl.ANY)
    out = pl.pallas_call(
        functools.partial(kernel, n_rep, scale, grad_scale),
        name="window",
        out_shape=jax.ShapeDtypeStruct((4, 16, width), F32),
        in_specs=[smem, smem, anywhere, anywhere] + [vmem] * 5,
        out_specs=vmem,
        scratch_shapes=[shape for _, shape in scratch_of(n_rep)],
        compiler_params=pltpu.CompilerParams(collective_id=0, has_side_effects=True),
    )(
        step_count,
        first_fragment,
        tokens[0],
        targets[0],
        inner_weights[0],
        first_moment[0],
        second_moment[0],
        outer_weights,
        outer_velocity,
    )
    return out[:2], out[2:][None]


def solution(mesh):
    in_specs = (
        P("rep", None, "shard", None),
        P("rep", None, "shard", None),
        P("rep", None, "shard", None),
        P(None, "shard", None),
        P(None, "shard", None),
        P("rep", None, "shard", None),
        P("rep", None, "shard", None, None),
        P(),
        P(),
    )
    out_specs = (P(None, "shard", None), P("rep", None, "shard", None))
    return jax.shard_map(body, mesh=mesh, in_specs=in_specs, out_specs=out_specs, check_vma=False)
```

time: 262 us -> 80.3 us (0.31)
  waiting for transfers between devices: 162 us -> 0 us
  Pallas kernels: 0 us -> 76.6 us
  starting transfers between devices: 68.3 us -> 0 us
  local copies, waits for them, and re-layouts: 16.7 us -> 1.53 us
  matrix products: 5.5 us -> 0 us
  other arithmetic: 4.07 us -> 0 us
    all_to_all x8 -> x0, waiting for transfers between devices: 162 us -> none  [the longest x6 106 us: from_everyone(): lax.all_to_all(jnp.broadcast_to(x[None], (peers, *x.shape)), axis, 0, 0,...]
    pallas_call x0 -> x1, Pallas kernels: none -> 76.6 us  [body(): pl.pallas_call(functools.partial(kernel, n_rep, scale, grad_scale), name=...]
    all_to_all x8 -> x0, starting transfers between devices: 68.3 us -> none  [the longest x6 53.5 us: from_everyone(): lax.all_to_all(jnp.broadcast_to(x[None], (peers, *x.shape)), axis, 0, 0,...]
    dot_general x2 -> x0, matrix products: 5.5 us -> none  [body(): jnp.einsum('tfk,td->fkd', residual, batch, preferred_element_type=jnp.flo...]
    broadcast_in_dim x6 -> x1, local copies, waits for them, and re-layouts: 6.39 us -> 1.53 us  [body(): return (out[:2], out[2:][None])]
    unnamed x17 -> x0, local copies, waits for them, and re-layouts: 4.58 us -> none
    slice x1 -> x0, local copies, waits for them, and re-layouts: 3.47 us -> none  [body(): target = targets[0, step]]
    reduce_sum x8 -> x0, other arithmetic: 2.96 us -> none  [the longest x4 1.34 us: of_everyone(): return jnp.sum(everything, axis=0)]
  transfers between devices with their start and end apart: 8 -> 0, of which waited for: 8 -> 0; matrix products, arithmetic and copies ran while one was open for 3% -> 0% of each run, Pallas kernels for 0% -> 0%
where the time goes in v2:
time: 80.3 us; the launch traced here: 80 us
  Pallas kernels  76.6 us (95%)
  between operations  1.93 us (2%)
  local copies, waits for them, and re-layouts  1.53 us (2%)
    pallas_call x1, Pallas kernels, body(): pl.pallas_call(functools.partial(kernel, n_rep, scale, grad_scale), name=...  76.6 us

profile of v2, /device:TPU:1, one launch (start us, length us, event | category | flops | bytes accessed | tf_op | source)
XLA Modules:
  0.0 80.0 jit_solution(11080583410562764104)
XLA Ops:
  1.9 76.6 %window.1 = f32[4,16,512]{2,1,0:T(8,128)} custom-call(s32[1]{0:T(128)S(6)} %copy.11.count_ref, s32[1]{0:T(128)S(6)} %copy.12.first_ref, bf16[2,512,512]{2,1,0:T(8,128)(2,1)} %bitcast.8, bf16[2,512,2,512]{3,2,1,0:T(2,128)(2,1)} %bitcast.7, f32[2,16,512]{2,1,0:T(8,128)} %bitcast.9, f32[2,16,512]{2,1,0:T(8,128)} %bitcast.10, f32[2,16,512]{2,1,0:T(8,128)} %bitcast.11, ...), custom_call_target="tpu_custom_call" | custom-call | tf_op jit(solution)/shard_map/window/pallas_call | solution.py:521
  78.5 1.5 %slice_bitcast_fusion = (f32[1,2,16,512]{3,2,1,0:T(8,128)}, f32[2,16,512]{2,1,0:T(8,128)}) fusion(f32[4,16,512]{2,1,0:T(8,128)} %window.1), kind=kLoop, calls=%fused_computation | loop fusion | bytes 262144 | tf_op jit(solution)/shard_map/broadcast_in_dim | solution.py:540

commit v3 on v2

--- a/solution.py
+++ b/solution.py
@@ -78,9 +78,11 @@
                     self.copy(d, i, u).wait_send()
 
 
-def kernel(n_rep, scale, grad_scale, count_ref, first_ref, x_hbm, t_hbm, w_ref, m_ref, v_ref, outer_ref, vel_ref, out_ref, *scratch):
+def kernel(n_rep, scale, grad_scale, count_ref, first_ref, x_hbm, t_hbm, w_hbm, m_hbm, v_hbm, outer_hbm, vel_hbm, out_ref, *scratch):
     names, shapes = zip(*scratch_of(n_rep))
     r = dict(zip(names, scratch, strict=True))
+    state = (w_hbm, m_hbm, v_hbm, outer_hbm, vel_hbm)
+    w_ref, m_ref, v_ref, outer_ref, vel_ref = (r["state"].at[i] for i in range(5))
     rep = lax.axis_index("rep")
     me = lax.axis_index("shard")
     z = me // 4
@@ -104,9 +106,8 @@
 
     barrier = pltpu.get_barrier_semaphore()
 
-    @pl.loop(1, NS)
-    def _(o):
-        pl.semaphore_signal(barrier, inc=1, device_id=(rep, (me + o) % NS), device_id_type=MESH)
+    for dev in (partner, at((z + 1) % NZ, y, k), at((z + NZ - 1) % NZ, y, k), across):
+        pl.semaphore_signal(barrier, inc=1, device_id=dev, device_id_type=MESH)
 
     @pl.loop(1, n_rep)
     def _(o):
@@ -118,9 +119,13 @@
             pltpu.make_async_copy(t_hbm.at[s], r["t"].at[s], r["load"].at[s, 1]),
         )
 
-    for s in range(2):
-        for c in load(s):
-            c.start()
+    def load_state(i):
+        return pltpu.make_async_copy(state[i], r["state"].at[i], r["load_state"].at[i])
+
+    for c in load(0):
+        c.start()
+    for i in range(5):
+        load_state(i).start()
 
     rep_out, rep_in, rep_all = r["rep_out"], r["rep_in"], r["rep_all"]
 
@@ -175,25 +180,31 @@
 
     def gram_rows(s, first_row):
         x = r["x"][s]
-        g = tdot(x, x).astype(BF16).reshape(NZ, NK, 32, 512)
+        xt = x.T
+        g = jnp.dot(xt, x, preferred_element_type=F32).astype(BF16).reshape(NZ, NK, 32, 512)
         for kk in range(NK):
             r["pa"][kk, :, pl.ds(first_row, 32), :] = g[:, kk]
-
-    for c in load(0):
-        c.wait()
-    gram_rows(0, 64)
+        return xt
+
+    load(0)[0].wait()
+    xt = gram_rows(0, 64)
+    load(0)[1].wait()
+    for c in load(1):
+        c.start()
     flat = r["t"][0].reshape(512, 1024)
     for kk in range(NK):
-        ct = tdot(r["x"][0], flat[:, 512 * kk : 512 * kk + 512])
+        ct = jnp.dot(xt, flat[:, 512 * kk : 512 * kk + 512], preferred_element_type=F32)
         r["pa"][kk, :, pl.ds(0, 64), :] = ct.astype(BF16).reshape(NZ, 64, 512)
+    for i in range(5):
+        load_state(i).wait()
+    w, m, v = w_ref[...], m_ref[...], v_ref[...]
+    r["wb"][...] = w.astype(BF16)
+    r["wall"][z, k] = r["wb"][k]
     for c in load(1):
         c.wait()
     gram_rows(1, 96)
-    w, m, v = w_ref[...], m_ref[...], v_ref[...]
-    r["wb"][...] = w.astype(BF16)
-    r["wall"][z, k] = r["wb"][k]
-
-    pl.semaphore_wait(barrier, NS - 1 + n_rep - 1)
+
+    pl.semaphore_wait(barrier, 4 + n_rep - 1)
     core_a().start()
 
     def w_swap():
@@ -214,23 +225,29 @@
 
     w_swap().start()
     lead = first_ref[0] == 0
-    rep_start(0, jnp.where(lead, w[0], w[1]))
-
+
+    w_step(0)
+    core_a().wait_recv()
+    ring_a.step(0)
+    w_step(1)
     flat = r["t"][1].reshape(512, 1024)
     for kk in range(NK):
-        c1 = tdot(flat[:, 512 * kk : 512 * kk + 512], r["x"][1])
-        r["pb"][kk] = c1.astype(BF16).reshape(NZ, 64, 512)
+        r["pb"][kk] = tdot(flat[:, 512 * kk : 512 * kk + 512], r["x"][1]).astype(BF16).reshape(NZ, 64, 512)
     core_b().start()
+    ring_a.step(1)
+    w_step(2)
+    rep_start(0, jnp.where(lead, w[0], w[1]))
+    ring_a.step(2)
+    w_step(3)
     row = lax.broadcasted_iota(jnp.int32, (512, 256), 0)
     col = lax.broadcasted_iota(jnp.int32, (512, 256), 1)
     place = jnp.where((row // 64 == col // 32) & (row % 32 == col % 32), (row // 32) % 2, 2)
     pick_mine = jnp.where(place == y, 1.0, 0.0).astype(BF16)
     pick_other = jnp.where(place == 1 - y, 1.0, 0.0).astype(BF16)
 
-    core_a().wait_recv()
-    for t in range(4):
-        ring_a.step(t)
-        w_step(t)
+    ring_a.step(3)
+    core_b().wait_recv()
+    ring_b.step(0)
 
     def y_copy(i):
         name = ("yc", "yg0", "yg1")[i]
@@ -245,12 +262,13 @@
     y_copy(1).start()
     r["yg1_out"][...] = r["ta"][pl.ds(96, 32), :].astype(BF16)
     y_copy(2).start()
+    ring_b.step(1)
     rep_middle(0)
-    core_b().wait_recv()
-    ring_b.step(0)
     cross = jnp.dot(hi, pick_mine, preferred_element_type=F32) + jnp.dot(lo, pick_mine, preferred_element_type=F32)
     w_copy(0, 3, (z + NZ - 4) % NZ).wait_recv()
     w_copy(1, 2, (z + 3) % NZ).wait_recv()
+
+    ring_b.step(2)
 
     def g0_swap(kk):
         return remote(r["gcol"].at[kk], r["gcol"].at[kk], r["gsw_s"], r["gsw_r"], partner)
@@ -260,6 +278,7 @@
     y_copy(1).wait_recv()
     r["gcol"][k] = (r["ta"][pl.ds(64, 32), :] + r["yg0_in"][...].astype(F32)).astype(BF16)
     g0_swap(k).start()
+    ring_b.step(3)
 
     def ag_copy(o, src):
         return remote(
@@ -272,6 +291,11 @@
 
     y_copy(2).wait_recv()
     r["gram"][z, k] = (r["ta"][pl.ds(96, 32), :] + r["yg1_in"][...].astype(F32)).astype(BF16)
+
+
+    for o in (4, 3, 5, 2, 6, 1, 7):
+        ag_copy(o, z).start()
+    fw_copy(0, k).start()
 
     def a_copy(o):
         to = (q + o) % 16
@@ -317,19 +341,6 @@
     def _(o):
         a_copy(o).start()
 
-    for o in (4, 3, 5, 2, 6, 1, 7):
-        ag_copy(o, z).start()
-    fw_copy(0, k).start()
-    ring_b.step(1)
-    ring_b.step(2)
-    for o in (1, 7, 2, 6):
-        ag_copy(o, (z + NZ - o) % NZ).wait_recv()
-        fw_copy(o, k).start()
-    ring_b.step(3)
-    for o in (3, 5, 4):
-        ag_copy(o, (z + NZ - o) % NZ).wait_recv()
-        fw_copy(o, k).start()
-
     ring_b.finish(r["tb"])
     peers = ((0, 1 - k), (1, k), (1, 1 - k))
 
@@ -343,6 +354,10 @@
         yy = y if dy == 0 else 1 - y
         r["c_out"][i] = r["tb"][pl.ds(yy * 32 + kk * 16, 16), :].astype(BF16)
         c_copy(i).start()
+
+    for o in (1, 7, 2, 6, 3, 5, 4):
+        ag_copy(o, (z + NZ - o) % NZ).wait_recv()
+        fw_copy(o, k).start()
 
     def adam(s, w, m, v, clipped):
         count = jnp.full((1, 8, 128), count_ref[0].astype(F32) + s, F32)
@@ -468,6 +483,8 @@
         ("rep_out", vmem((2, n_rep, 1, D), F32)),
         ("rep_in", vmem((2, n_rep, 1, D), F32)),
         ("rep_all", vmem((2, n_rep, 1, D), F32)),
+        ("state", vmem((5, 2, 16, D), F32)),
+        ("load_state", dma((5,))),
         ("load", dma((2, 2))),
         ("core_s", dma((2,))),
         ("core_r", dma((2,))),
@@ -522,7 +539,7 @@
         functools.partial(kernel, n_rep, scale, grad_scale),
         name="window",
         out_shape=jax.ShapeDtypeStruct((4, 16, width), F32),
-        in_specs=[smem, smem, anywhere, anywhere] + [vmem] * 5,
+        in_specs=[smem, smem] + [anywhere] * 7,
         out_specs=vmem,
         scratch_shapes=[shape for _, shape in scratch_of(n_rep)],
         compiler_params=pltpu.CompilerParams(collective_id=0, has_side_effects=True),

time: 80.3 us -> 69 us (0.86)
  Pallas kernels: 76.6 us -> 65.3 us
    pallas_call x1, Pallas kernels: 76.6 us -> 65.3 us  [body(): pl.pallas_call(functools.partial(kernel, n_rep, scale, grad_scale), name=...]
where the time goes in v3:
time: 69 us; the launch traced here: 68.7 us
  Pallas kernels  65.3 us (95%)
  between operations  1.93 us (3%)
  local copies, waits for them, and re-layouts  1.53 us (2%)
    pallas_call x1, Pallas kernels, body(): pl.pallas_call(functools.partial(kernel, n_rep, scale, grad_scale), name=...  65.3 us
    broadcast_in_dim x1, local copies, waits for them, and re-layouts, body(): return (out[:2], out[2:][None])  1.53 us

profile of v3, /device:TPU:1, one launch (start us, length us, event | category | flops | bytes accessed | tf_op | source)
XLA Modules:
  0.0 68.7 jit_solution(9760255165297731974)
XLA Ops:
  1.9 65.3 %window.1 = f32[4,16,512]{2,1,0:T(8,128)} custom-call(s32[1]{0:T(128)S(6)} %copy.11.count_ref, s32[1]{0:T(128)S(6)} %copy.12.first_ref, bf16[2,512,512]{2,1,0:T(8,128)(2,1)} %bitcast.8, bf16[2,512,2,512]{3,2,1,0:T(2,128)(2,1)} %bitcast.7, f32[2,16,512]{2,1,0:T(8,128)} %bitcast.9, f32[2,16,512]{2,1,0:T(8,128)} %bitcast.10, f32[2,16,512]{2,1,0:T(8,128)} %bitcast.11, ...), custom_call_target="tpu_custom_call" | custom-call | tf_op jit(solution)/shard_map/window/pallas_call | solution.py:538
  67.2 1.5 %slice_bitcast_fusion = (f32[1,2,16,512]{3,2,1,0:T(8,128)}, f32[2,16,512]{2,1,0:T(8,128)}) fusion(f32[4,16,512]{2,1,0:T(8,128)} %window.1), kind=kLoop, calls=%fused_computation | loop fusion | bytes 262144 | tf_op jit(solution)/shard_map/broadcast_in_dim | solution.py:557

commit v4 on v3

--- a/solution.py
+++ b/solution.py
@@ -104,15 +104,6 @@
             src_ref=src, dst_ref=dst, send_sem=ss, recv_sem=rs, device_id=dev, device_id_type=MESH
         )
 
-    barrier = pltpu.get_barrier_semaphore()
-
-    for dev in (partner, at((z + 1) % NZ, y, k), at((z + NZ - 1) % NZ, y, k), across):
-        pl.semaphore_signal(barrier, inc=1, device_id=dev, device_id_type=MESH)
-
-    @pl.loop(1, n_rep)
-    def _(o):
-        pl.semaphore_signal(barrier, inc=1, device_id=((rep + o) % n_rep, me), device_id_type=MESH)
-
     def load(s):
         return (
             pltpu.make_async_copy(x_hbm.at[s], r["x"].at[s], r["load"].at[s, 0]),
@@ -126,6 +117,15 @@
         c.start()
     for i in range(5):
         load_state(i).start()
+
+    barrier = pltpu.get_barrier_semaphore()
+
+    for dev in (partner, at((z + 1) % NZ, y, k), at((z + NZ - 1) % NZ, y, k), across):
+        pl.semaphore_signal(barrier, inc=1, device_id=dev, device_id_type=MESH)
+
+    @pl.loop(1, n_rep)
+    def _(o):
+        pl.semaphore_signal(barrier, inc=1, device_id=((rep + o) % n_rep, me), device_id_type=MESH)
 
     rep_out, rep_in, rep_all = r["rep_out"], r["rep_in"], r["rep_all"]
 
@@ -400,16 +400,6 @@
     g = (prod * scale - r["c1"][...].reshape(32, 512)) * grad_scale
     norm_start(1, g)
     rep_middle(1)
-    clipped = g.reshape(2, 16, 512) * clip_factor(1)
-    w, m, v = adam(1, w, m, v, clipped)
-    theta1 = outer_step(
-        jnp.where(lead, outer_ref[1], outer_ref[0]), jnp.where(lead, vel_ref[1], vel_ref[0]), rep_end(1)
-    )
-    out_ref[0] = jnp.where(lead, theta0, theta1)
-    out_ref[1] = jnp.where(lead, theta1, theta0)
-    out_ref[2] = jnp.where(lead, w[0], mixing * theta1 + (1.0 - mixing) * w[0])
-    out_ref[3] = jnp.where(lead, mixing * theta1 + (1.0 - mixing) * w[1], w[1])
-
     core_a().wait_send()
     core_b().wait_send()
     ring_a.drain()
@@ -431,8 +421,7 @@
     def _(o):
         a_copy(o).wait_send()
 
-    for s in range(2):
-
+    def drain_sums(s):
         @pl.loop(1, NS)
         def _(o):
             n_copy(s, o).wait_send()
@@ -442,8 +431,21 @@
             rep_send_copy(s, o).wait_send()
             rep_back_copy(s, o, rep).wait_send()
 
-
-SUB_A, SUB_B = 32, 32
+    drain_sums(0)
+    clipped = g.reshape(2, 16, 512) * clip_factor(1)
+    w, m, v = adam(1, w, m, v, clipped)
+    theta1 = outer_step(
+        jnp.where(lead, outer_ref[1], outer_ref[0]), jnp.where(lead, vel_ref[1], vel_ref[0]), rep_end(1)
+    )
+    out_ref[0] = jnp.where(lead, theta0, theta1)
+    out_ref[1] = jnp.where(lead, theta1, theta0)
+    out_ref[2] = jnp.where(lead, w[0], mixing * theta1 + (1.0 - mixing) * w[0])
+    out_ref[3] = jnp.where(lead, mixing * theta1 + (1.0 - mixing) * w[1], w[1])
+
+    drain_sums(1)
+
+
+SUB_A, SUB_B = 64, 32
 
 
 def scratch_of(n_rep):

time: 69 us -> 67.2 us (0.974)
  Pallas kernels: 65.3 us -> 63.6 us
    pallas_call x1, Pallas kernels: 65.3 us -> 63.6 us  [body(): pl.pallas_call(functools.partial(kernel, n_rep, scale, grad_scale), name=...]
where the time goes in v4:
time: 67.2 us; the launch traced here: 67 us
  Pallas kernels  63.6 us (95%)
  between operations  1.93 us (3%)
  local copies, waits for them, and re-layouts  1.53 us (2%)
    pallas_call x1, Pallas kernels, body(): pl.pallas_call(functools.partial(kernel, n_rep, scale, grad_scale), name=...  63.6 us
    broadcast_in_dim x1, local copies, waits for them, and re-layouts, body(): return (out[:2], out[2:][None])  1.53 us

profile of v4, /device:TPU:1, one launch (start us, length us, event | category | flops | bytes accessed | tf_op | source)
XLA Modules:
  0.0 67.0 jit_solution(17088610759162974353)
XLA Ops:
  1.9 63.6 %window.1 = f32[4,16,512]{2,1,0:T(8,128)} custom-call(s32[1]{0:T(128)S(6)} %copy.11.count_ref, s32[1]{0:T(128)S(6)} %copy.12.first_ref, bf16[2,512,512]{2,1,0:T(8,128)(2,1)} %bitcast.8, bf16[2,512,2,512]{3,2,1,0:T(2,128)(2,1)} %bitcast.7, f32[2,16,512]{2,1,0:T(8,128)} %bitcast.9, f32[2,16,512]{2,1,0:T(8,128)} %bitcast.10, f32[2,16,512]{2,1,0:T(8,128)} %bitcast.11, ...), custom_call_target="tpu_custom_call" | custom-call | tf_op jit(solution)/shard_map/window/pallas_call | solution.py:540
  65.5 1.5 %slice_bitcast_fusion = (f32[1,2,16,512]{3,2,1,0:T(8,128)}, f32[2,16,512]{2,1,0:T(8,128)}) fusion(f32[4,16,512]{2,1,0:T(8,128)} %window.1), kind=kLoop, calls=%fused_computation | loop fusion | bytes 262144 | tf_op jit(solution)/shard_map/broadcast_in_dim | solution.py:559
